TPU v7x, 256 devices: a whole 4x4x8 slice. The times are simulated.
256 devices in a mesh: rows: 32 (over y, z), tensor: 8 (over x, core).
Axes of the slice: x: 4, y: 4, z: 8, core: 2. Of those that a mesh axis runs over, the one named last changes fastest.
Arguments:
- token_ids: int32 [256, 4], replicated, may hold values from 0 to 65535
- cache_lengths: int32 [256], P('rows'), may hold values from 160 to 1280, as said below
- doc_ids: int32 [256], replicated, may hold values from 0 to 31
- embed_table: bfloat16 [65536, 8192], P('tensor', 'rows'), may hold values from -10.5 to 10.5
- cache_keys: bfloat16 [256, 1280, 1024], P('rows', None, 'tensor'), may hold values from -700 to 700
- cache_values: bfloat16 [256, 1280, 1024], P('rows', None, 'tensor'), may hold values from -6 to 6
- decode_gain: float32 [8192], P('rows'), may hold values from 0.1 to 1.9
- decode_query: bfloat16 [8192, 8192], P('rows', 'tensor'), may hold values from -0.0625 to 0.0625
- decode_key: bfloat16 [8192, 1024], P('rows', 'tensor'), may hold values from -0.0625 to 0.0625
- decode_value: bfloat16 [8192, 1024], P('rows', 'tensor'), may hold values from -0.0625 to 0.0625
- decode_out: bfloat16 [8192, 8192], P('tensor', 'rows'), may hold values from -0.0625 to 0.0625
- reduce_gain: float32 [8192], P('rows'), may hold values from 0.8 to 10
- reduce_query: bfloat16 [8192, 8192], P('rows', 'tensor'), may hold values from -0.0625 to 0.0625
- reduce_key: bfloat16 [8192, 1024], P('rows', 'tensor'), may hold values from -0.0625 to 0.0625
- reduce_value: bfloat16 [8192, 1024], P('rows', 'tensor'), may hold values from -0.0625 to 0.0625
- reduce_out: bfloat16 [8192, 8192], P('tensor', 'rows'), may hold values from -0.0625 to 0.0625
Outputs:
- reduced: bfloat16 [1024, 8192], P(None, 'rows')
Inputs may be any that keep to these rules, and one draw needn't show every extreme that they name: Passage row c holds cache entries at positions below cache_lengths[c]; one row in every draw has a full cache of 1280.
All inputs are finite; a program needn't handle non-finite values.
Results may differ from a plain program's by a relative error of at most 0.035.
The roundings to bfloat16 on the way count: a program that leaves them out, or rounds other values in their place, can miss the bound.
Values may be sent and summed in bfloat16 or wider, within the bound.
A program may use at most 64 MiB of HBM per device.

v0:
```python
import jax
import jax.numpy as jnp
from jax import lax
from jax.sharding import PartitionSpec as P

D = 8192
HEAD_DIM = 128
EPSILON = 1e-05
ROPE_BASE = 500000.0


def rotate(vectors, positions):
    half_dim = vectors.shape[-1] // 2
    frequencies = ROPE_BASE ** (-2.0 * jnp.arange(half_dim, dtype=jnp.float32) / vectors.shape[-1])
    angles = positions.astype(jnp.float32)[..., None] * frequencies
    cosine = jnp.cos(angles)
    sine_part = jnp.sin(angles)
    lower_half = vectors[..., :half_dim]
    upper_half = vectors[..., half_dim:]
    return jnp.concatenate(
        [
            lower_half * cosine - upper_half * sine_part,
            upper_half * cosine + lower_half * sine_part,
        ],
        axis=-1,
    )


def width_total(partial_value):
    return lax.psum(partial_value, "tensor")


def row_scale(squares):
    summed = lax.psum(squares, "rows")
    return lax.rsqrt(summed / D + EPSILON)


def head_terms(normed, matrices):
    return lax.psum_scatter(
        jnp.concatenate(
            [jnp.dot(normed, matrix, preferred_element_type=jnp.float32) for matrix in matrices],
            axis=1,
        ),
        "rows",
        scatter_dimension=0,
        tiled=True,
    )


def head_mix(attended, matrix):
    return jnp.dot(
        lax.all_gather(attended, "rows", axis=0, tiled=True),
        matrix,
        preferred_element_type=jnp.float32,
    )


def per_device(
    token_ids,
    cache_lengths,
    doc_ids,
    embed_table,
    cache_keys,
    cache_values,
    decode_gain,
    decode_query,
    decode_key,
    decode_value,
    decode_out,
    reduce_gain,
    reduce_query,
    reduce_key,
    reduce_value,
    reduce_out,
):
    step_count = token_ids.shape[1]
    passage_count = token_ids.shape[0]
    token_count = passage_count * step_count
    own_passages = cache_lengths.shape[0]
    own_tokens = own_passages * step_count
    row_first = lax.axis_index("rows") * own_tokens
    query_cols = decode_query.shape[1]
    kv_cols = decode_key.shape[1]
    local_heads = query_cols // HEAD_DIM
    local_kv = kv_cols // HEAD_DIM
    group_size = local_heads // local_kv
    score_scale = HEAD_DIM ** (-0.5)
    step_ids = jnp.arange(step_count, dtype=jnp.int32)
    vocab_part = embed_table.shape[0]
    local_ids = token_ids.reshape(token_count) - lax.axis_index("tensor") * vocab_part
    inside = (local_ids >= 0) & (local_ids < vocab_part)
    picked = jnp.take(embed_table, jnp.clip(local_ids, 0, vocab_part - 1), axis=0)
    picked = jnp.where(inside[:, None], picked.astype(jnp.float32), 0.0)
    embedded = width_total(picked)
    dec_scale = row_scale(jnp.sum(embedded * embedded, axis=1))
    normed = (embedded * decode_gain[None, :]).astype(jnp.bfloat16)
    projected = head_terms(normed, (decode_query, decode_key, decode_value))
    projected = projected * lax.dynamic_slice_in_dim(dec_scale, row_first, own_tokens, 0)[:, None]
    positions = (cache_lengths[:, None] + step_ids[None, :]).reshape(own_tokens, 1)
    queries = rotate(
        projected[:, :query_cols].reshape(own_tokens, local_heads, HEAD_DIM), positions
    ).astype(jnp.bfloat16)
    keys_new = rotate(
        projected[:, query_cols : query_cols + kv_cols].reshape(own_tokens, local_kv, HEAD_DIM),
        positions,
    ).astype(jnp.bfloat16)
    values_new = projected[:, query_cols + kv_cols :].astype(jnp.bfloat16)
    queries = queries.reshape(own_passages, step_count, local_kv, group_size, HEAD_DIM)
    keys_new = keys_new.reshape(own_passages, step_count, local_kv, HEAD_DIM)
    values_new = values_new.reshape(own_passages, step_count, local_kv, HEAD_DIM)
    capacity = cache_keys.shape[1]
    keys_old = cache_keys.reshape(own_passages, capacity, local_kv, HEAD_DIM)
    values_old = cache_values.reshape(own_passages, capacity, local_kv, HEAD_DIM)
    new_scores = (
        jnp.einsum("rskgd,rtkd->rskgt", queries, keys_new, preferred_element_type=jnp.float32)
        * score_scale
    )
    causal = step_ids[None, :] <= step_ids[:, None]
    new_scores = jnp.where(causal[None, :, None, None, :], new_scores, -jnp.inf)
    old_scores = (
        jnp.einsum("rskgd,rckd->rskgc", queries, keys_old, preferred_element_type=jnp.float32)
        * score_scale
    )
    slot_ids = jnp.arange(capacity, dtype=jnp.int32)
    live_mask = slot_ids[None, :] < cache_lengths[:, None]
    old_scores = jnp.where(live_mask[:, None, None, None, :], old_scores, -jnp.inf)
    highest = jnp.maximum(jnp.max(old_scores, axis=-1), jnp.max(new_scores, axis=-1))
    old_exp = jnp.exp(old_scores - highest[..., None])
    new_exp = jnp.exp(new_scores - highest[..., None])
    summed = jnp.sum(old_exp, axis=-1) + jnp.sum(new_exp, axis=-1)
    old_weights = (old_exp / summed[..., None]).astype(jnp.bfloat16)
    new_weights = (new_exp / summed[..., None]).astype(jnp.bfloat16)
    attended = jnp.einsum(
        "rskgc,rckd->rskgd", old_weights, values_old, preferred_element_type=jnp.float32
    )
    attended = attended + jnp.einsum(
        "rskgt,rtkd->rskgd", new_weights, values_new, preferred_element_type=jnp.float32
    )
    attended = attended.reshape(own_tokens, query_cols).astype(jnp.bfloat16)
    partial_value = head_mix(attended, decode_out)
    summary = (embedded + width_total(partial_value)).astype(jnp.bfloat16)
    summary_wide = summary.astype(jnp.float32)
    red_scale = row_scale(jnp.sum(summary_wide * summary_wide, axis=1))
    normed_red = (summary_wide * reduce_gain[None, :]).astype(jnp.bfloat16)
    passage_index = jnp.arange(passage_count, dtype=jnp.int32)
    earlier = jnp.sum(
        (
            (doc_ids[None, :] == doc_ids[:, None])
            & (passage_index[None, :] < passage_index[:, None])
        ).astype(jnp.int32),
        axis=1,
    )
    doc_positions = (earlier[:, None] * step_count + step_ids[None, :]).reshape(token_count, 1)
    doc_tokens = (doc_ids[:, None] + jnp.zeros_like(step_ids)[None, :]).reshape(token_count)
    own_positions = lax.dynamic_slice_in_dim(doc_positions, row_first, own_tokens, 0)
    own_scale = lax.dynamic_slice_in_dim(red_scale, row_first, own_tokens, 0)[:, None]
    projected = head_terms(normed_red, (reduce_query, reduce_key, reduce_value)) * own_scale
    queries_red = rotate(
        projected[:, :query_cols].reshape(own_tokens, local_heads, HEAD_DIM), own_positions
    ).astype(jnp.bfloat16)
    keys_own = (
        rotate(
            projected[:, query_cols : query_cols + kv_cols].reshape(own_tokens, local_kv, HEAD_DIM),
            own_positions,
        )
        .astype(jnp.bfloat16)
        .reshape(own_tokens, kv_cols)
    )
    values_own = projected[:, query_cols + kv_cols :].astype(jnp.bfloat16)
    keys_red, values_red = (
        lax.all_gather(keys_own, "rows", axis=0, tiled=True),
        lax.all_gather(values_own, "rows", axis=0, tiled=True),
    )
    queries_red = queries_red.reshape(own_tokens, local_kv, group_size, HEAD_DIM)
    keys_red = keys_red.reshape(token_count, local_kv, HEAD_DIM)
    values_red = values_red.reshape(token_count, local_kv, HEAD_DIM)
    token_index = jnp.arange(token_count, dtype=jnp.int32)
    own_index = row_first + jnp.arange(own_tokens, dtype=jnp.int32)
    own_docs = lax.dynamic_slice_in_dim(doc_tokens, row_first, own_tokens, 0)
    allowed = (own_docs[:, None] == doc_tokens[None, :]) & (
        token_index[None, :] <= own_index[:, None]
    )
    red_scores = (
        jnp.einsum("tkgd,ukd->tkgu", queries_red, keys_red, preferred_element_type=jnp.float32)
        * score_scale
    )
    red_scores = jnp.where(allowed[:, None, None, :], red_scores, -jnp.inf)
    red_high = jnp.max(red_scores, axis=-1)
    red_exp = jnp.exp(red_scores - red_high[..., None])
    red_weights = (red_exp / jnp.sum(red_exp, axis=-1)[..., None]).astype(jnp.bfloat16)
    red_out = jnp.einsum(
        "tkgu,ukd->tkgd", red_weights, values_red, preferred_element_type=jnp.float32
    )
    red_out = red_out.reshape(own_tokens, query_cols).astype(jnp.bfloat16)
    return (summary_wide + width_total(head_mix(red_out, reduce_out))).astype(jnp.bfloat16)


def solution(mesh):
    return jax.shard_map(
        per_device,
        mesh=mesh,
        in_specs=(
            P(),
            P("rows"),
            P(),
            P("tensor", "rows"),
            P("rows", None, "tensor"),
            P("rows", None, "tensor"),
            P("rows"),
            P("rows", "tensor"),
            P("rows", "tensor"),
            P("rows", "tensor"),
            P("tensor", "rows"),
            P("rows"),
            P("rows", "tensor"),
            P("rows", "tensor"),
            P("rows", "tensor"),
            P("tensor", "rows"),
        ),
        out_specs=P(None, "rows"),
        check_vma=False,
    )
```

profile of v0, /device:TPU:8, one launch (start us, length us, event | category | flops | bytes accessed | tf_op | source)
XLA Modules:
  0.0 966.4 jit_solution(12764112662389864731)
XLA Ops:
  6.5 0.8 subtract_clamp_fusion
  7.8 0.7 compare_and_fusion.1
  8.8 6.2 gather_fusion
  15.0 1.3 convert_select_fusion
  16.4 70.6 %all-reduce.4.cloned.1.call-done = f32[1024,256]{1,0:T(8,128)} async-done(((f32[1024,256]{1,0:T(8,128)}), f32[1024,256]{1,0:T(8,128)}) %all-reduce.4.cloned.1.call-update) | async-done | bytes 1048592 | tf_op jit(solution)/shard_map/psum | solution.py:30
  87.1 1.4 multiply_reduce_fusion
  88.6 0.8 fusion.72
  90.0 2.8 pad_maximum_fusion
  92.8 5.9 copy.69
  98.8 0.6 copy-done.7
  100.4 63.5 %psum.36 = f32[1024]{0:T(1024)S(1)} all-reduce(f32[1024]{0:T(1024)S(1)} %get-tuple-element.7), channel_id=1, replica_groups=mesh['rows'=32,'tensor'=8] {'rows'}, use_global_device_ids=true, to_apply=%region_3.4 | all-reduce | flops 1024 | bytes 8192 | tf_op jit(solution)/shard_map/psum | solution.py:34
  164.0 160.3 %reduce-scatter.7.cloned.1.call-done = f32[32,1280]{1,0:T(8,128)} async-done(((f32[1024,1280]{1,0:T(8,128)}), f32[32,1280]{1,0:T(8,128)}) %reduce-scatter.7.cloned.1.call-update) | async-done | bytes 163856 | tf_op jit(solution)/shard_map/reduce_scatter | solution.py:39
  324.2 1.0 broadcast_multiply_fusion.1
  325.6 1.1 fusion.69
  328.5 0.6 copy.86
  329.2 75.8 %all-gather.3.cloned.1.call-done = bf16[1024,1024]{1,0:T(8,128)(2,1)} async-done(((bf16[32,1024]{1,0:T(8,128)(2,1)}), bf16[1024,1024]{1,0:T(8,128)(2,1)}) %all-gather.3.cloned.1.call-update) | async-done | bytes 2097168 | tf_op jit(solution)/shard_map/all_gather | solution.py:52
  405.0 3.3 fusion.75
  408.3 66.2 %all-reduce.6.cloned.1.call-done = f32[1024,256]{1,0:T(8,128)} async-done(((f32[1024,256]{1,0:T(8,128)}), f32[1024,256]{1,0:T(8,128)}) %all-reduce.6.cloned.1.call-update) | async-done | bytes 1048592 | tf_op jit(solution)/shard_map/psum | solution.py:30
  474.6 1.8 fusion.22
  476.4 1.8 fusion.32
  478.9 2.8 pad_maximum_fusion.1
  481.6 5.9 copy.71
  488.0 63.5 %psum.38 = f32[1024]{0:T(1024)S(1)} all-reduce(f32[1024]{0:T(1024)S(1)} %get-tuple-element.5), channel_id=1, replica_groups=mesh['rows'=32,'tensor'=8] {'rows'}, use_global_device_ids=true, to_apply=%region_11.12 | all-reduce | flops 1024 | bytes 8192 | tf_op jit(solution)/shard_map/psum | solution.py:34
  551.7 161.6 %reduce-scatter.9.cloned.1.call-done = f32[32,1280]{1,0:T(8,128)} async-done(((f32[1024,1280]{1,0:T(8,128)}), f32[32,1280]{1,0:T(8,128)}) %reduce-scatter.9.cloned.1.call-update) | async-done | bytes 163856 | tf_op jit(solution)/shard_map/reduce_scatter | solution.py:39
  713.2 1.0 broadcast_multiply_fusion
  714.5 47.5 %all_gather.14 = bf16[1024,128]{1,0:T(8,128)(2,1)S(1)} all-gather(bf16[32,128]{1,0:T(8,128)(2,1)S(1)} %pad_maximum_fusion.5), channel_id=1, replica_groups=mesh['rows'=32,'tensor'=8] {'rows'}, dimensions={0}, use_global_device_ids=true | all-gather | bytes 270336 | tf_op jit(solution)/shard_map/all_gather | solution.py:171
  762.1 47.8 %all_gather.13 = bf16[1024,128]{1,0:T(8,128)(2,1)S(1)} all-gather(bf16[32,128]{1,0:T(8,128)(2,1)S(1)} %slice.100), channel_id=1, replica_groups=mesh['rows'=32,'tensor'=8] {'rows'}, dimensions={0}, use_global_device_ids=true | all-gather | bytes 270336 | tf_op jit(solution)/shard_map/all_gather | solution.py:172
  811.2 0.6 copy.85
  811.9 75.9 %all-gather.5.cloned.1.call-done = bf16[1024,1024]{1,0:T(8,128)(2,1)} async-done(((bf16[32,1024]{1,0:T(8,128)(2,1)}), bf16[1024,1024]{1,0:T(8,128)(2,1)}) %all-gather.5.cloned.1.call-update) | async-done | bytes 2097168 | tf_op jit(solution)/shard_map/all_gather | solution.py:52
  887.7 3.4 fusion.76
  891.1 66.3 %all-reduce.8.cloned.1.call-done = f32[1024,256]{1,0:T(8,128)} async-done(((f32[1024,256]{1,0:T(8,128)}), f32[1024,256]{1,0:T(8,128)}) %all-reduce.8.cloned.1.call-update) | async-done | bytes 1048592 | tf_op jit(solution)/shard_map/psum | solution.py:30
  957.4 2.1 fusion.23
  (94 shorter events, 7.5 us)
Async XLA Ops:
  6.5 319.0 %copy-start = (bf16[8,1280,128]{2,1,0:T(8,128)(2,1)S(1)}, bf16[8,1280,128]{2,1,0:T(8,128)(2,1)}, u32[]{:S(2)}) copy-start(bf16[8,1280,128]{2,1,0:T(8,128)(2,1)} %param.20) | copy-start | bytes 7864324
  6.5 80.5 %all-reduce.4.cloned.1.call-start = ((), (), s32[]{:S(2)}) async-start(), calls=%async_computation.2 | async-start | bytes 2097152 | tf_op jit(solution)/shard_map/psum | solution.py:30
  8.8 78.3 %copy-start.9 = (f32[256]{0:T(256)S(1)}, f32[256]{0:T(256)}, u32[]{:S(2)}) copy-start(f32[256]{0:T(256)} %param.22) | copy-start | bytes 3076
  16.4 72.2 %copy-start.1 = (bf16[256,1024]{1,0:T(8,128)(2,1)S(1)}, bf16[256,1024]{1,0:T(8,128)(2,1)}, u32[]{:S(2)}) copy-start(bf16[256,1024]{1,0:T(8,128)(2,1)} %param.23) | copy-start | bytes 1572868
  16.4 307.8 %reduce-scatter.7.cloned.1.call-start = ((), (), s32[]{:S(2)}) async-start(), calls=%async_computation.7 | async-start | bytes 5406720 | tf_op jit(solution)/shard_map/reduce_scatter | solution.py:39
  88.5 0.8 copy-start.2
  88.5 1.1 copy-start.3
  98.7 0.7 copy-start.7
  98.7 1.1 copy-start.8
  98.8 306.2 %all-gather.3.cloned.1.call-start = ((), (), s32[]{:S(2)}) async-start(), calls=%async_computation.3 | async-start | bytes 2162688 | tf_op jit(solution)/shard_map/all_gather | solution.py:52
  325.6 2.3 copy-start.10
  327.9 77.1 %copy-start.11 = (bf16[1024,256]{1,0:T(8,128)(2,1)S(1)}, bf16[1024,256]{1,0:T(8,128)(2,1)}, u32[]{:S(2)}) copy-start(bf16[1024,256]{1,0:T(8,128)(2,1)} %param.26) | copy-start | bytes 1572868
  329.1 145.4 %all-reduce.6.cloned.1.call-start = ((), (), s32[]{:S(2)}) async-start(), calls=%async_computation.4 | async-start | bytes 2097152 | tf_op jit(solution)/shard_map/psum | solution.py:30
  408.3 68.1 %copy-start.6 = (f32[256]{0:T(256)S(1)}, f32[256]{0:T(256)}, u32[]{:S(2)}) copy-start(f32[256]{0:T(256)} %param.27) | copy-start | bytes 3076
  408.3 305.0 %reduce-scatter.9.cloned.1.call-start = ((), (), s32[]{:S(2)}) async-start(), calls=%async_computation.8 | async-start | bytes 5406720 | tf_op jit(solution)/shard_map/reduce_scatter | solution.py:39
  476.3 1.9 copy-start.4
  476.3 2.2 copy-start.5
  487.6 400.1 %all-gather.5.cloned.1.call-start = ((), (), s32[]{:S(2)}) async-start(), calls=%async_computation.5 | async-start | bytes 2162688 | tf_op jit(solution)/shard_map/all_gather | solution.py:52
  811.8 145.6 %all-reduce.8.cloned.1.call-start = ((), (), s32[]{:S(2)}) async-start(), calls=%async_computation.6 | async-start | bytes 2097152 | tf_op jit(solution)/shard_map/psum | solution.py:30
Sparse Core Ops, SparseCore 0:
  16.5 70.5 all-reduce.3
  98.9 225.3 reduce-scatter.6
  329.3 75.6 all-gather.2
  408.4 66.1 all-reduce.5
  487.7 225.4 reduce-scatter.8
  811.9 75.7 all-gather.4
  891.3 66.1 all-reduce.7
where the time goes:
time: 967 us; the launch traced here: 966 us
  waiting for transfers between devices  677 us (70%)
  blocking collectives  222 us (23%)
  local copies, waits for them, and re-layouts  21.6 us (2%)
  other arithmetic  17.9 us (2%)
  between operations  13.9 us (1%)
  matrix products  13.7 us (1%)
    reduce_scatter x2, waiting for transfers between devices, head_terms(): lax.psum_scatter(jnp.concatenate([jnp.dot(normed, matrix, preferred_eleme...  322 us
    psum x3, waiting for transfers between devices, width_total(): return lax.psum(partial_value, 'tensor')  203 us
    all_gather x2, waiting for transfers between devices, head_mix(): lax.all_gather(attended, 'rows', axis=0, tiled=True)  152 us
    psum x2, blocking collectives, row_scale(): summed = lax.psum(squares, 'rows')  127 us
    all_gather x1, blocking collectives, per_device(): lax.all_gather(values_own, 'rows', axis=0, tiled=True)  47.8 us
    all_gather x1, blocking collectives, per_device(): lax.all_gather(keys_own, 'rows', axis=0, tiled=True)  47.5 us
  transfers between devices with their start and end apart: 7, of which 7 were waited for; matrix products, arithmetic and copies ran while one was open for 0% of the time, Pallas kernels for 0%

commit v1 on v0

--- a/solution.py
+++ b/solution.py
@@ -7,6 +7,12 @@
 HEAD_DIM = 128
 EPSILON = 1e-05
 ROPE_BASE = 500000.0
+
+
+def gather_from_all(x, axis, dim):
+    size = lax.axis_size(axis)
+    repeats = [size if d == dim else 1 for d in range(x.ndim)]
+    return lax.all_to_all(jnp.tile(x, repeats), axis, split_axis=dim, concat_axis=dim, tiled=True)
 
 
 def rotate(vectors, positions):
@@ -169,7 +175,7 @@
     values_own = projected[:, query_cols + kv_cols :].astype(jnp.bfloat16)
     keys_red, values_red = (
         lax.all_gather(keys_own, "rows", axis=0, tiled=True),
-        lax.all_gather(values_own, "rows", axis=0, tiled=True),
+        gather_from_all(values_own, "rows", 0),
     )
     queries_red = queries_red.reshape(own_tokens, local_kv, group_size, HEAD_DIM)
     keys_red = keys_red.reshape(token_count, local_kv, HEAD_DIM)

time: 967 us -> 932 us (0.964)
  blocking collectives: 222 us -> 176 us
    all_gather x1 -> x0, blocking collectives: 47.8 us -> none  [per_device(): lax.all_gather(values_own, 'rows', axis=0, tiled=True)]
  transfers between devices with their start and end apart: 7 -> 8, of which waited for: 7 -> 7; matrix products, arithmetic and copies ran while one was open for 0% -> 0% of each run, Pallas kernels for 0% -> 0%
where the time goes in v1:
time: 932 us; the launch traced here: 931 us
  waiting for transfers between devices  677 us (73%)
  blocking collectives  176 us (19%)
  local copies, waits for them, and re-layouts  23.3 us (2%)
  other arithmetic  17.9 us (2%)
  matrix products  15 us (2%)
  between operations  13.9 us (1%)
    reduce_scatter x2, waiting for transfers between devices, head_terms(): lax.psum_scatter(jnp.concatenate([jnp.dot(normed, matrix, preferred_eleme...  322 us
    psum x3, waiting for transfers between devices, width_total(): return lax.psum(partial_value, 'tensor')  203 us
    all_gather x2, waiting for transfers between devices, head_mix(): lax.all_gather(attended, 'rows', axis=0, tiled=True)  152 us
    psum x2, blocking collectives, row_scale(): summed = lax.psum(squares, 'rows')  127 us
    all_gather x1, blocking collectives, per_device(): lax.all_gather(keys_own, 'rows', axis=0, tiled=True)  48.8 us
  transfers between devices with their start and end apart: 8, of which 7 were waited for; matrix products, arithmetic and copies ran while one was open for 0% of the time, Pallas kernels for 0%

profile of v1, /device:TPU:8, one launch (start us, length us, event | category | flops | bytes accessed | tf_op | source)
XLA Modules:
  0.0 931.1 jit_solution(5877527530287394735)
XLA Ops:
  6.5 0.8 subtract_clamp_fusion
  7.8 0.7 compare_and_fusion.1
  8.8 6.2 gather_fusion
  15.0 1.3 convert_select_fusion
  16.4 70.6 %all-reduce.4.cloned.1.call-done = f32[1024,256]{1,0:T(8,128)} async-done(((f32[1024,256]{1,0:T(8,128)}), f32[1024,256]{1,0:T(8,128)}) %all-reduce.4.cloned.1.call-update) | async-done | bytes 1048592 | tf_op jit(solution)/shard_map/psum | solution.py:36
  87.1 1.4 multiply_reduce_fusion
  88.6 0.8 fusion.71
  90.0 2.8 pad_maximum_fusion
  92.8 5.9 copy.69
  100.4 63.5 %psum.36 = f32[1024]{0:T(1024)S(1)} all-reduce(f32[1024]{0:T(1024)S(1)} %get-tuple-element.7), channel_id=1, replica_groups=mesh['rows'=32,'tensor'=8] {'rows'}, use_global_device_ids=true, to_apply=%region_3.4 | all-reduce | flops 1024 | bytes 8192 | tf_op jit(solution)/shard_map/psum | solution.py:40
  164.0 160.3 %reduce-scatter.7.cloned.1.call-done = f32[32,1280]{1,0:T(8,128)} async-done(((f32[1024,1280]{1,0:T(8,128)}), f32[32,1280]{1,0:T(8,128)}) %reduce-scatter.7.cloned.1.call-update) | async-done | bytes 163856 | tf_op jit(solution)/shard_map/reduce_scatter | solution.py:45
  324.2 1.0 broadcast_multiply_fusion.1
  325.6 1.1 fusion.68
  329.2 75.8 %all-gather.3.cloned.1.call-done = bf16[1024,1024]{1,0:T(8,128)(2,1)} async-done(((bf16[32,1024]{1,0:T(8,128)(2,1)}), bf16[1024,1024]{1,0:T(8,128)(2,1)}) %all-gather.3.cloned.1.call-update) | async-done | bytes 2097168 | tf_op jit(solution)/shard_map/all_gather | solution.py:58
  405.0 3.3 fusion.74
  408.3 66.2 %all-reduce.6.cloned.1.call-done = f32[1024,256]{1,0:T(8,128)} async-done(((f32[1024,256]{1,0:T(8,128)}), f32[1024,256]{1,0:T(8,128)}) %all-reduce.6.cloned.1.call-update) | async-done | bytes 1048592 | tf_op jit(solution)/shard_map/psum | solution.py:36
  474.6 1.8 fusion.22
  476.4 1.8 fusion.32
  478.9 2.8 pad_maximum_fusion.1
  481.6 5.9 copy.71
  488.0 63.6 %psum.38 = f32[1024]{0:T(1024)S(1)} all-reduce(f32[1024]{0:T(1024)S(1)} %get-tuple-element.5), channel_id=1, replica_groups=mesh['rows'=32,'tensor'=8] {'rows'}, use_global_device_ids=true, to_apply=%region_11.12 | all-reduce | flops 1024 | bytes 8192 | tf_op jit(solution)/shard_map/psum | solution.py:40
  551.6 161.4 %reduce-scatter.9.cloned.1.call-done = f32[32,1280]{1,0:T(8,128)} async-done(((f32[1024,1280]{1,0:T(8,128)}), f32[32,1280]{1,0:T(8,128)}) %reduce-scatter.9.cloned.1.call-update) | async-done | bytes 163856 | tf_op jit(solution)/shard_map/reduce_scatter | solution.py:45
  713.0 1.0 broadcast_multiply_fusion
  714.3 0.7 tile.2
  715.1 7.9 all-to-all-start
  723.2 48.8 %all_gather.10 = bf16[1024,128]{1,0:T(8,128)(2,1)S(1)} all-gather(bf16[32,128]{1,0:T(8,128)(2,1)S(1)} %pad_maximum_fusion.5), channel_id=1, replica_groups=mesh['rows'=32,'tensor'=8] {'rows'}, dimensions={0}, use_global_device_ids=true | all-gather | bytes 270336 | tf_op jit(solution)/shard_map/all_gather | solution.py:177
  772.4 1.0 copy-done.1
  773.7 1.7 fusion.18
  776.1 76.4 %all-gather.5.cloned.1.call-done = bf16[1024,1024]{1,0:T(8,128)(2,1)} async-done(((bf16[32,1024]{1,0:T(8,128)(2,1)}), bf16[1024,1024]{1,0:T(8,128)(2,1)}) %all-gather.5.cloned.1.call-update) | async-done | bytes 2097168 | tf_op jit(solution)/shard_map/all_gather | solution.py:58
  852.5 3.4 fusion.75
  855.9 66.3 %all-reduce.8.cloned.1.call-done = f32[1024,256]{1,0:T(8,128)} async-done(((f32[1024,256]{1,0:T(8,128)}), f32[1024,256]{1,0:T(8,128)}) %all-reduce.8.cloned.1.call-update) | async-done | bytes 1048592 | tf_op jit(solution)/shard_map/psum | solution.py:36
  922.1 2.1 fusion.23
  (98 shorter events, 9.0 us)
Async XLA Ops:
  6.5 319.0 %copy-start = (bf16[8,1280,128]{2,1,0:T(8,128)(2,1)S(1)}, bf16[8,1280,128]{2,1,0:T(8,128)(2,1)}, u32[]{:S(2)}) copy-start(bf16[8,1280,128]{2,1,0:T(8,128)(2,1)} %param.20) | copy-start | bytes 7864324
  6.5 80.5 %all-reduce.4.cloned.1.call-start = ((), (), s32[]{:S(2)}) async-start(), calls=%async_computation.3 | async-start | bytes 2097152 | tf_op jit(solution)/shard_map/psum | solution.py:36
  8.8 78.3 %copy-start.10 = (f32[256]{0:T(256)S(1)}, f32[256]{0:T(256)}, u32[]{:S(2)}) copy-start(f32[256]{0:T(256)} %param.22) | copy-start | bytes 3076
  16.4 72.2 %copy-start.2 = (bf16[256,1024]{1,0:T(8,128)(2,1)S(1)}, bf16[256,1024]{1,0:T(8,128)(2,1)}, u32[]{:S(2)}) copy-start(bf16[256,1024]{1,0:T(8,128)(2,1)} %param.23) | copy-start | bytes 1572868
  16.4 307.8 %reduce-scatter.7.cloned.1.call-start = ((), (), s32[]{:S(2)}) async-start(), calls=%async_computation.8 | async-start | bytes 5406720 | tf_op jit(solution)/shard_map/reduce_scatter | solution.py:45
  88.5 0.8 copy-start.3
  88.5 1.1 copy-start.4
  98.7 0.7 copy-start.8
  98.7 1.1 copy-start.9
  98.8 306.2 %all-gather.3.cloned.1.call-start = ((), (), s32[]{:S(2)}) async-start(), calls=%async_computation.4 | async-start | bytes 2162688 | tf_op jit(solution)/shard_map/all_gather | solution.py:58
  325.6 2.3 copy-start.11
  327.9 77.1 %copy-start.12 = (bf16[1024,256]{1,0:T(8,128)(2,1)S(1)}, bf16[1024,256]{1,0:T(8,128)(2,1)}, u32[]{:S(2)}) copy-start(bf16[1024,256]{1,0:T(8,128)(2,1)} %param.26) | copy-start | bytes 1572868
  329.1 145.4 %all-reduce.6.cloned.1.call-start = ((), (), s32[]{:S(2)}) async-start(), calls=%async_computation.5 | async-start | bytes 2097152 | tf_op jit(solution)/shard_map/psum | solution.py:36
  408.3 68.1 %copy-start.7 = (f32[256]{0:T(256)S(1)}, f32[256]{0:T(256)}, u32[]{:S(2)}) copy-start(f32[256]{0:T(256)} %param.27) | copy-start | bytes 3076
  408.3 304.7 %reduce-scatter.9.cloned.1.call-start = ((), (), s32[]{:S(2)}) async-start(), calls=%async_computation.9 | async-start | bytes 5406720 | tf_op jit(solution)/shard_map/reduce_scatter | solution.py:45
  476.3 1.9 copy-start.5
  476.3 2.2 copy-start.6
  715.1 58.6 %all-to-all-start = ((bf16[32,32,128]{2,1,0:T(8,128)(2,1)}), bf16[32,32,128]{2,1,0:T(8,128)(2,1)}, u32[]{:S(2)}, u32[]{:S(2)}) async-start(bf16[32,32,128]{2,1,0:T(8,128)(2,1)} %tile.2), calls=%async_computation | async-start | bytes 524288 | tf_op jit(solution)/shard_map/all_to_all | solution.py:15
  723.0 129.5 %all-gather.5.cloned.1.call-start = ((), (), s32[]{:S(2)}) async-start(), calls=%async_computation.6 | async-start | bytes 2162688 | tf_op jit(solution)/shard_map/all_gather | solution.py:58
  772.4 1.0 copy-start.1
  776.1 146.1 %all-reduce.8.cloned.1.call-start = ((), (), s32[]{:S(2)}) async-start(), calls=%async_computation.7 | async-start | bytes 2097152 | tf_op jit(solution)/shard_map/psum | solution.py:36
Sparse Core Ops, SparseCore 0:
  16.5 70.5 all-reduce.3
  98.9 225.3 reduce-scatter.6
  329.3 75.6 all-gather.2
  408.4 66.1 all-reduce.5
  487.7 225.2 reduce-scatter.8
  776.2 76.2 all-gather.4
  856.0 66.0 all-reduce.7
